TPU v7x, 128 devices: a whole 4x4x4 slice. The times are simulated.
128 devices in a mesh: stn: 8 (over x_hi, y), tm: 16 (over x_lo, z, core).
Axes of the slice: x: 4 (x_hi: 2, x_lo: 2; x = x_hi * 2 + x_lo), y: 4, z: 4, core: 2. Of those that a mesh axis runs over, the one named last changes fastest.
Arguments:
- voltages: bfloat16 [512, 256, 4096], P('stn', 'tm'), may hold values from -52 to 52
- pfb_taps: float32 [16, 4096], replicated, may hold values from -1.5 to 1.5
- eq_gains: float32 [512, 2048], P('stn'), may hold values from 0.5 to 11
Outputs:
- visibilities: float32 [2048, 512, 512], P(('stn', 'tm'))
All inputs are finite; a program needn't handle non-finite values.
Results may differ from a plain program's by a relative error of at most 0.0014.
Values may be sent and summed in bfloat16 or wider, within the bound.
No kernel may reach another device: no remote copies, remote signals or barrier semaphores. Data moves between devices by JAX's collectives and lax.ppermute only.
A program may use at most 448 MiB of HBM per device.

v0:
```python
import math
import jax
import jax.numpy as jnp
from jax import lax
from jax.sharding import PartitionSpec as P


def from_behind(value, axis, steps):
    count = lax.axis_size(axis)
    first, last = (max(0, -steps), min(count, count - steps))
    return lax.ppermute(value, axis, [(source, source + steps) for source in range(first, last)])


def cos_sin(numer, denom):
    angle = 2.0 * math.pi / denom * (numer % denom).astype(jnp.float32)
    return (jnp.cos(angle), jnp.sin(angle))


def transform(filtered, channels):
    inputs_dev, frames_dev, length = filtered.shape
    inner_len = 64
    outer_len = length // inner_len
    kept_upper = channels // outer_len
    row_count = inputs_dev * frames_dev
    highest = lax.Precision.HIGHEST
    arranged = filtered.reshape(row_count, outer_len, inner_len)
    freq_one = lax.broadcasted_iota(jnp.int32, (outer_len, outer_len), 0)
    time_one = lax.broadcasted_iota(jnp.int32, (outer_len, outer_len), 1)
    cos_one, sin_one = cos_sin(freq_one * time_one, outer_len)
    section_one = jnp.stack([cos_one, -sin_one])
    partial_ft = jnp.einsum("qka,Rab->qkbR", section_one, arranged, precision=highest)
    freq_twist = lax.broadcasted_iota(jnp.int32, (outer_len, inner_len), 0)
    time_twist = lax.broadcasted_iota(jnp.int32, (outer_len, inner_len), 1)
    twist_cos, twist_sin = cos_sin(freq_twist * time_twist, length)
    twist_table = jnp.stack([jnp.stack([twist_cos, twist_sin]), jnp.stack([-twist_sin, twist_cos])])
    freq_two = lax.broadcasted_iota(jnp.int32, (kept_upper, inner_len), 0)
    time_two = lax.broadcasted_iota(jnp.int32, (kept_upper, inner_len), 1)
    cos_two, sin_two = cos_sin(freq_two * time_two, inner_len)
    section_two = jnp.stack(
        [jnp.stack([cos_two, sin_two], axis=1), jnp.stack([-sin_two, cos_two], axis=1)]
    )
    combined = jnp.einsum("qjrb,rskb->qjksb", section_two, twist_table, precision=highest)
    spectrum = jnp.einsum("qjksb,skbR->qjkR", combined, partial_ft, precision=highest)
    return spectrum.reshape(2, channels, row_count)


def per_device(voltages, pfb_taps, eq_gains):
    tap_count = pfb_taps.shape[0]
    history_len = tap_count - 1
    inputs_dev, frames_dev, length = voltages.shape
    channels = eq_gains.shape[1]
    station_groups = lax.axis_size("stn")
    time_groups = lax.axis_size("tm")
    per_group = channels // (station_groups * time_groups)
    all_inputs = inputs_dev * station_groups
    all_frames = frames_dev * time_groups
    earlier = from_behind(voltages[:, frames_dev - history_len :, :], "tm", 1)
    extended = jnp.concatenate([earlier, voltages], axis=1).astype(jnp.float32)
    kernel = jnp.flip(pfb_taps, axis=0)[:, None, :]
    filtered = lax.conv_general_dilated(
        extended,
        kernel,
        (1,),
        "VALID",
        dimension_numbers=("NWC", "WIO", "NWC"),
        feature_group_count=length,
        precision=lax.Precision.HIGHEST,
    )
    spectrum = transform(filtered, channels)
    gains_turned = jnp.transpose(eq_gains)
    spectra = (
        spectrum.reshape(2, channels, inputs_dev, frames_dev) * gains_turned[None, :, :, None]
    ).astype(jnp.bfloat16)
    shaped = spectra.reshape(2, station_groups * time_groups, per_group, inputs_dev * frames_dev)
    turned = lax.all_to_all(shaped, ("stn", "tm"), split_axis=1, concat_axis=1, tiled=True)
    blocks = turned.reshape(2, station_groups, time_groups, per_group, inputs_dev, frames_dev)
    columns = jnp.transpose(blocks, (0, 3, 1, 4, 2, 5)).reshape(
        2, per_group, all_inputs, all_frames
    )
    swapped = jnp.stack([columns[1], -columns[0]])
    vis_real = jnp.einsum("rcnt,rcmt->cnm", columns, columns, preferred_element_type=jnp.float32)
    vis_imag = jnp.einsum("rcnt,rcmt->cnm", swapped, columns, preferred_element_type=jnp.float32)
    local_power = jnp.sum(jnp.diagonal(vis_real, axis1=1, axis2=2), axis=0)
    power = lax.psum(local_power, ("stn", "tm"))
    scale = lax.rsqrt(power / (all_frames * channels) + 1e-06)
    weight = scale[:, None] * scale[None, :] / all_frames
    row_ids = lax.broadcasted_iota(jnp.int32, (all_inputs, all_inputs), 0)
    col_ids = lax.broadcasted_iota(jnp.int32, (all_inputs, all_inputs), 1)
    lower = row_ids >= col_ids
    return jnp.where(lower[None], vis_real, vis_imag) * weight[None]


def solution(mesh):
    in_specs = (P("stn", "tm", None), P(), P("stn", None))
    out_specs = P(("stn", "tm"), None, None)
    return jax.shard_map(
        per_device, mesh=mesh, in_specs=in_specs, out_specs=out_specs, check_vma=False
    )
```

profile of v0, /device:TPU:1, one launch (start us, length us, event | category | flops | bytes accessed | tf_op | source)
XLA Modules:
  0.0 891.8 jit_solution(8095447733145545676)
XLA Ops:
  0.0 11.4 %copy.46 = bf16[64,16,4096]{2,0,1:T(8,128)(2,1)} copy(bf16[64,16,4096]{2,1,0:T(8,128)(2,1)} %param.3) | data formatting | bytes 16777216 | tf_op args[0]
  11.4 7.4 slice.19
  18.8 5.1 collective-permute-start
  23.8 0.1 fusion.37
  24.0 0.1 fusion.33
  24.2 0.1 copy.70
  24.3 0.1 fusion.40
  24.4 0.1 fusion.38
  24.5 0.1 copy.71
  24.7 5.3 convolution_bitcast_fusion.2
  29.9 6.8 copy.54
  36.7 0.5 rev.4
  37.2 0.3 copy.56
  37.6 21.5 %mul.180 = f32[2048,64,16]{2,1,0:T(8,128)} broadcast(f32[2048,64]{1,0:T(8,128)S(1)} %copy.56), dimensions={0,1} | broadcast | bytes 8912896 | tf_op jit(solution)/shard_map/mul | solution.py:72
  59.0 54.5 %mul.181 = f32[128,16,1024]{2,1,0:T(8,128)} reshape(f32[2048,64,16]{2,1,0:T(8,128)} %mul.180) | data formatting | bytes 16777216 | tf_op jit(solution)/shard_map/mul | solution.py:72
  113.5 0.8 sine_negate_fusion
  114.3 0.0 collective-permute-done
  114.3 22.0 %fusion.3 = f32[64,16,4096]{2,0,1:T(8,128)S(1)} fusion(bf16[64,16,4096]{2,0,1:T(8,128)(2,1)} %copy.46, bf16[64,15,4096]{2,0,1:T(8,128)(2,1)} %collective-permute-done, f32[16,1,4096]{2,0,1:T(8,128)S(1)} %bitcast.69), kind=kOutput, calls=%fused_computation.6 | convolution fusion | flops 813432832 | bytes 33292288 | tf_op jit(solution)/shard_map/conv_general_dilated | solution.py:60
  136.4 18.8 %copy.49 = f32[64,16,4096]{2,1,0:T(8,128)} copy(f32[64,16,4096]{2,0,1:T(8,128)S(1)} %fusion.3) | data formatting | bytes 33554432 | tf_op jit(solution)/shard_map/conv_general_dilated | solution.py:60
  155.2 27.0 %reshape.234 = f32[1024,64,64]{2,1,0:T(8,128)} reshape(f32[64,16,4096]{2,1,0:T(8,128)} %copy.49) | data formatting | bytes 33554432 | tf_op jit(solution)/shard_map/reshape | solution.py:26
  182.2 26.2 %copy.69 = f32[1024,64,64,1]{0,1,3,2:T(8,128)} copy(f32[1024,64,64,1]{2,1,0,3:T(8,128)} %bitcast.62) | data formatting | bytes 33554432 | tf_op jit(solution)/shard_map/reshape | solution.py:26
  208.4 33.7 %convolution_bitcast_fusion = f32[2,64,64,1024,1]{3,1,0,2,4:T(8,128)} fusion(f32[1024,64,64,1]{0,1,3,2:T(8,128)} %copy.69, f32[1,64,64]{2,1,0:T(8,128)S(1)} %copy-done.5, f32[1,64,64]{2,1,0:T(8,128)S(1)} %copy-done.6), kind=kOutput, calls=%fused_computation.10 | convolution fusion | flops 6442459136 | bytes 50364416 | tf_op jit(solution)/shard_map/qka,Rab->qkbR/dot_general | solution.py:31
  242.1 47.6 %fusion.7 = f32[2,32,64,1024]{3,1,0,2:T(8,128)} fusion(f32[2,32,64,2,64]{4,1,3,0,2:T(8,128)S(1)} %copy-done.1, f32[2,64,64,1024,1]{3,1,0,2,4:T(8,128)} %convolution_bitcast_fusion), kind=kOutput, calls=%fused_computation.11 | convolution fusion | flops 6442450944 | bytes 52428800 | tf_op jit(solution)/shard_map/qjksb,skbR->qjkR/dot_general | solution.py:43
  289.7 15.6 %copy.55 = f32[2,32,64,1024]{3,2,1,0:T(8,128)S(1)} copy(f32[2,32,64,1024]{3,1,0,2:T(8,128)} %fusion.7) | data formatting | bytes 33554432 | tf_op jit(solution)/shard_map/qjksb,skbR->qjkR/transpose | solution.py:43
  305.3 5.1 multiply_convert_fusion
  310.5 8.5 copy.57
  319.0 10.1 %all-to-all-start = ((bf16[2,128,16,1024]{3,2,0,1:T(8,128)(2,1)}), bf16[2,128,16,1024]{3,2,0,1:T(8,128)(2,1)}, u32[]{:S(2)}, u32[]{:S(2)}) async-start(bf16[2,128,16,1024]{3,2,0,1:T(8,128)(2,1)} %copy.57), calls=%async_computation | async-start | bytes 16777216 | tf_op jit(solution)/shard_map/all_to_all | solution.py:75
  329.1 0.5 shift-left_or_fusion
  329.6 0.8 iota_compare_fusion
  330.4 100.1 %all-to-all-done = bf16[2,128,16,1024]{3,2,0,1:T(8,128)(2,1)} async-done(((bf16[2,128,16,1024]{3,2,0,1:T(8,128)(2,1)}), bf16[2,128,16,1024]{3,2,0,1:T(8,128)(2,1)}, u32[]{:S(2)}, u32[]{:S(2)}) %all-to-all-start) | async-done | bytes 8388640 | tf_op jit(solution)/shard_map/all_to_all | solution.py:75
  430.5 62.1 %reshape.251 = bf16[2,8,16,16,64,16]{5,4,3,0,2,1:T(8,128)(2,1)} reshape(bf16[2,128,16,1024]{3,2,0,1:T(8,128)(2,1)} %all-to-all-done) | data formatting | bytes 16777216 | tf_op jit(solution)/shard_map/reshape | solution.py:76
  492.6 56.9 %copy.59 = bf16[2,8,16,16,64,16]{4,5,2,1,3,0:T(8,128)(2,1)} copy(bf16[2,8,16,16,64,16]{5,4,3,0,2,1:T(8,128)(2,1)} %reshape.251) | data formatting | bytes 16777216 | tf_op jit(solution)/shard_map/reshape | solution.py:76
  549.5 57.9 %copy.60 = bf16[2,16,8,64,16,16]{3,2,5,4,1,0:T(8,128)(2,1)} copy(bf16[2,16,8,64,16,16]{5,3,1,0,4,2:T(8,128)(2,1)} %bitcast.18) | data formatting | bytes 16777216 | tf_op jit(solution)/shard_map/transpose | solution.py:77
  607.4 22.5 %reshape.236 = bf16[2,16,512,256]{2,3,1,0:T(8,128)(2,1)} reshape(bf16[2,16,8,64,16,16]{3,2,5,4,1,0:T(8,128)(2,1)} %copy.60) | data formatting | bytes 16777216 | tf_op jit(solution)/shard_map/reshape | solution.py:77
  629.9 16.5 %convolution_bitcast_fusion.1 = f32[16,512,512]{2,1,0:T(8,128)} fusion(bf16[2,16,512,256]{2,3,1,0:T(8,128)(2,1)} %reshape.236), kind=kOutput, calls=%fused_computation.12 | convolution fusion | flops 4294967296 | bytes 25165824 | tf_op jit(solution)/shard_map/rcnt,rcmt->cnm/dot_general | solution.py:81
  646.3 11.7 %fusion.44 = (bf16[1,16,8,64,16,16]{3,5,4,2,1,0:T(8,128)(2,1)}, bf16[1,16,8,64,16,16]{3,5,4,2,1,0:T(8,128)(2,1)}) fusion(bf16[2,16,8,64,16,16]{3,5,4,2,1,0:T(8,128)(2,1)} %bitcast.63), kind=kLoop, calls=%fused_computation.70 | loop fusion | flops 2097152 | bytes 16777216 | tf_op jit(solution)/shard_map/slice | solution.py:80
  658.0 20.2 %copy.64 = bf16[1,16,8,64,16,16]{3,2,5,4,1,0:T(8,128)(2,1)} copy(bf16[1,16,8,64,16,16]{3,5,4,2,1,0:T(8,128)(2,1)} %get-tuple-element.6) | data formatting | bytes 8388608 | tf_op jit(solution)/shard_map/neg | solution.py:80
  678.2 11.8 %neg.47 = bf16[1,16,512,256]{2,3,1,0:T(8,128)(2,1)} reshape(bf16[1,16,8,64,16,16]{3,2,5,4,1,0:T(8,128)(2,1)} %copy.64) | data formatting | bytes 8388608 | tf_op jit(solution)/shard_map/neg | solution.py:80
  690.1 6.3 copy.66
  696.4 20.2 %copy.63 = bf16[1,16,8,64,16,16]{3,2,5,4,1,0:T(8,128)(2,1)} copy(bf16[1,16,8,64,16,16]{3,5,4,2,1,0:T(8,128)(2,1)} %get-tuple-element.5) | data formatting | bytes 8388608 | tf_op jit(solution)/shard_map/slice | solution.py:80
  716.6 11.8 %slice.15 = bf16[1,16,512,256]{2,3,1,0:T(8,128)(2,1)} reshape(bf16[1,16,8,64,16,16]{3,2,5,4,1,0:T(8,128)(2,1)} %copy.63) | data formatting | bytes 8388608 | tf_op jit(solution)/shard_map/slice | solution.py:80
  728.4 6.3 copy.65
  734.8 62.4 %copy.68 = f32[16,512,512]{0,2,1:T(8,128)} copy(f32[16,512,512]{2,1,0:T(8,128)} %convolution_bitcast_fusion.1) | data formatting | bytes 33554432 | tf_op jit(solution)/shard_map/rcnt,rcmt->cnm/dot_general | solution.py:81
  797.1 5.5 gather_fusion
  802.6 0.1 reduce_sum.9
  802.8 69.5 %psum.7 = f32[512]{0:T(512)S(1)} all-reduce(f32[512]{0:T(512)S(1)} %reduce_sum.9), channel_id=1, replica_groups=mesh['stn'=8,'tm'=16] {'stn','tm'}, use_global_device_ids=true, to_apply=%region_1.2 | all-reduce | flops 512 | bytes 4096 | tf_op jit(solution)/shard_map/psum | solution.py:84
  872.3 0.1 multiply_multiply_fusion
  872.5 18.9 %fusion.2 = f32[16,512,512]{2,1,0:T(8,128)} fusion(f32[16,512,512]{2,1,0:T(8,128)} %convolution_bitcast_fusion.1, bf16[1,16,512,256]{3,2,0,1:T(8,128)(2,1)} %copy.66, bf16[1,16,512,256]{3,2,0,1:T(8,128)(2,1)} %copy.65, bf16[2,16,512,256]{2,3,1,0:T(8,128)(2,1)} %reshape.236, f32[512,512]{1,0:T(8,128)S(1)} %multiply_multiply_fusion, ...), kind=kOutput, calls=%fused_computation.4 | convolution fusion | flops 4307550208 | bytes 51642368 | tf_op jit(solution)/shard_map/rcnt,rcmt->cnm/dot_general | solution.py:82
  (24 shorter events, 0.1 us)
Async XLA Ops:
  18.8 18.0 %copy-start.4 = (f32[16,4096]{1,0:T(8,128)S(1)}, f32[16,4096]{1,0:T(8,128)}, u32[]{:S(2)}) copy-start(f32[16,4096]{1,0:T(8,128)} %param.4) | copy-start | bytes 786436
  18.8 18.5 %copy-start.3 = (f32[64,2048]{1,0:T(8,128)S(1)}, f32[64,2048]{1,0:T(8,128)}, u32[]{:S(2)}) copy-start(f32[64,2048]{1,0:T(8,128)} %param.5) | copy-start | bytes 1572868
  18.8 95.6 %collective-permute-start = (bf16[64,15,4096]{2,0,1:T(8,128)(2,1)}, bf16[64,15,4096]{2,0,1:T(8,128)(2,1)}, u32[]{:S(2)}, u32[]{:S(2)}) collective-permute-start(bf16[64,15,4096]{2,0,1:T(8,128)(2,1)} %slice.19), channel_id=1, source_target_pairs={{0,1},{1,2},{2,3},{3,4},{4,5},{5,6},{6,7},{7,8},{8,9},{9,10},{10,1... | collective-permute-start | bytes 23592968 | tf_op jit(solution)/shard_map/ppermute | solution.py:11
  182.2 26.2 %copy-start.5 = (f32[1,64,64]{2,1,0:T(8,128)S(1)}, f32[1,64,64]{2,1,0:T(8,128)}, u32[]{:S(2)}) copy-start(f32[1,64,64]{2,1,0:T(8,128)} %get-tuple-element.15) | copy-start | bytes 49156
  182.2 26.2 %copy-start.6 = (f32[1,64,64]{2,1,0:T(8,128)S(1)}, f32[1,64,64]{2,1,0:T(8,128)}, u32[]{:S(2)}) copy-start(f32[1,64,64]{2,1,0:T(8,128)} %get-tuple-element.16) | copy-start | bytes 49156
  208.4 33.7 %copy-start.1 = (f32[2,32,64,2,64]{4,1,3,0,2:T(8,128)S(1)}, f32[2,32,64,2,64]{4,1,3,0,2:T(8,128)}, u32[]{:S(2)}) copy-start(f32[2,32,64,2,64]{4,1,3,0,2:T(8,128)} %copy.54) | copy-start | bytes 6291460
  208.4 96.9 %slice-start = ((s8[8388608]{0:T(1024)(128)(4,1)}), s8[4194304]{0:T(1024)(128)(4,1)S(1)}, s32[]{:S(2)}) async-start(s8[8388608]{0:T(1024)(128)(4,1)} %bitcast.66), calls=%async_computation.1 | async-start | bytes 8388608
  242.1 63.2 %slice-start.1 = ((s8[8388608]{0:T(1024)(128)(4,1)}), s8[4194304]{0:T(1024)(128)(4,1)S(1)}, s32[]{:S(2)}) async-start(s8[8388608]{0:T(1024)(128)(4,1)} %bitcast.66), calls=%async_computation.2 | async-start | bytes 8388608
  319.0 111.6 %all-to-all-start = ((bf16[2,128,16,1024]{3,2,0,1:T(8,128)(2,1)}), bf16[2,128,16,1024]{3,2,0,1:T(8,128)(2,1)}, u32[]{:S(2)}, u32[]{:S(2)}) async-start(bf16[2,128,16,1024]{3,2,0,1:T(8,128)(2,1)} %copy.57), calls=%async_computation | async-start | bytes 16777216 | tf_op jit(solution)/shard_map/all_to_all | solution.py:75
  734.8 62.4 %copy-start = (s32[512,1]{0,1:T(1,128)S(1)}, s32[512,1]{0,1:T(1,128)}, u32[]{:S(2)}) copy-start(s32[512,1]{0,1:T(1,128)} %shift-left_or_fusion) | copy-start | bytes 6148
  734.8 137.7 %copy-start.2 = (pred[512,512]{1,0:T(8,128)(4,1)S(1)}, pred[512,512]{1,0:T(8,128)(4,1)}, u32[]{:S(2)}) copy-start(pred[512,512]{1,0:T(8,128)(4,1)} %iota_compare_fusion) | copy-start | bytes 786436
where the time goes:
time: 907 us; the launch traced here: 892 us
  local copies, waits for them, and re-layouts  543 us (60%)
  matrix products  144 us (16%)
  waiting for transfers between devices  100 us (11%)
  blocking collectives  69.5 us (8%)
  other arithmetic  19.7 us (2%)
  starting transfers between devices  15.2 us (2%)
    reshape x2, local copies, waits for them, and re-layouts, per_device(): turned.reshape(2, station_groups, time_groups, per_group, inputs_dev, fra...  119 us
    all_to_all x1, waiting for transfers between devices, per_device(): lax.all_to_all(shaped, ('stn', 'tm'), split_axis=1, concat_axis=1, tiled=...  100 us
    mul x2, local copies, waits for them, and re-layouts, per_device(): spectrum.reshape(2, channels, inputs_dev, frames_dev)  76 us
    psum x1, blocking collectives, per_device(): power = lax.psum(local_power, ('stn', 'tm'))  69.5 us
    dot_general x1, local copies, waits for them, and re-layouts, per_device(): jnp.einsum('rcnt,rcmt->cnm', columns, columns, preferred_element_type=jnp...  62.4 us
    transpose x1, local copies, waits for them, and re-layouts, per_device(): jnp.transpose(blocks, (0, 3, 1, 4, 2, 5))  57.9 us
    reshape x2, local copies, waits for them, and re-layouts, transform(): arranged = filtered.reshape(row_count, outer_len, inner_len)  53.2 us
    dot_general x1, matrix products, transform(): jnp.einsum('qjksb,skbR->qjkR', combined, partial_ft, precision=highest)  47.6 us
  transfers between devices with their start and end apart: 2, of which 1 were waited for; matrix products, arithmetic and copies ran while one was open for 10% of the time, Pallas kernels for 0%

commit v1 on v0

--- a/solution.py
+++ b/solution.py
@@ -81,7 +81,9 @@
     vis_real = jnp.einsum("rcnt,rcmt->cnm", columns, columns, preferred_element_type=jnp.float32)
     vis_imag = jnp.einsum("rcnt,rcmt->cnm", swapped, columns, preferred_element_type=jnp.float32)
     local_power = jnp.sum(jnp.diagonal(vis_real, axis1=1, axis2=2), axis=0)
-    power = lax.psum(local_power, ("stn", "tm"))
+    power = local_power
+    for mesh_axis in ("stn", "tm"):
+        power = lax.psum(power, mesh_axis)
     scale = lax.rsqrt(power / (all_frames * channels) + 1e-06)
     weight = scale[:, None] * scale[None, :] / all_frames
     row_ids = lax.broadcasted_iota(jnp.int32, (all_inputs, all_inputs), 0)

time: 907 us -> 889 us (0.980)
  blocking collectives: 69.5 us -> 51.9 us
    psum x1 -> x2, blocking collectives: 69.5 us -> 51.9 us  [per_device(): power = lax.psum(power, mesh_axis)]
  transfers between devices with their start and end apart: 2 -> 2, of which waited for: 1 -> 1; matrix products, arithmetic and copies ran while one was open for 10% -> 11% of each run, Pallas kernels for 0% -> 0%
where the time goes in v1:
time: 889 us; the launch traced here: 874 us
  local copies, waits for them, and re-layouts  542 us (61%)
  matrix products  144 us (16%)
  waiting for transfers between devices  100 us (11%)
  blocking collectives  51.9 us (6%)
  other arithmetic  19.8 us (2%)
  starting transfers between devices  15.2 us (2%)
    reshape x2, local copies, waits for them, and re-layouts, per_device(): turned.reshape(2, station_groups, time_groups, per_group, inputs_dev, fra...  119 us
    all_to_all x1, waiting for transfers between devices, per_device(): lax.all_to_all(shaped, ('stn', 'tm'), split_axis=1, concat_axis=1, tiled=...  100 us
    mul x2, local copies, waits for them, and re-layouts, per_device(): spectrum.reshape(2, channels, inputs_dev, frames_dev)  76 us
    dot_general x1, local copies, waits for them, and re-layouts, per_device(): jnp.einsum('rcnt,rcmt->cnm', columns, columns, preferred_element_type=jnp...  61.6 us
    transpose x1, local copies, waits for them, and re-layouts, per_device(): jnp.transpose(blocks, (0, 3, 1, 4, 2, 5))  57.9 us
    reshape x2, local copies, waits for them, and re-layouts, transform(): arranged = filtered.reshape(row_count, outer_len, inner_len)  53.3 us
    psum x2, blocking collectives, per_device(): power = lax.psum(power, mesh_axis)  51.9 us
    dot_general x1, matrix products, transform(): jnp.einsum('qjksb,skbR->qjkR', combined, partial_ft, precision=highest)  47.6 us
  transfers between devices with their start and end apart: 2, of which 1 were waited for; matrix products, arithmetic and copies ran while one was open for 11% of the time, Pallas kernels for 0%

profile of v1, /device:TPU:1, one launch (start us, length us, event | category | flops | bytes accessed | tf_op | source)
XLA Modules:
  0.0 873.5 jit_solution(9107597892418527830)
XLA Ops:
  0.0 11.4 %copy.46 = bf16[64,16,4096]{2,0,1:T(8,128)(2,1)} copy(bf16[64,16,4096]{2,1,0:T(8,128)(2,1)} %param.3) | data formatting | bytes 16777216 | tf_op args[0]
  11.4 7.4 slice.19
  18.8 5.1 collective-permute-start
  23.8 0.1 fusion.37
  24.0 0.1 fusion.33
  24.2 0.1 copy.70
  24.3 0.1 fusion.40
  24.4 0.1 fusion.38
  24.5 0.1 copy.71
  24.7 5.3 convolution_bitcast_fusion.2
  29.9 6.8 copy.54
  36.7 0.5 rev.4
  37.3 0.3 copy.56
  37.6 21.5 %mul.180 = f32[2048,64,16]{2,1,0:T(8,128)} broadcast(f32[2048,64]{1,0:T(8,128)S(1)} %copy.56), dimensions={0,1} | broadcast | bytes 8912896 | tf_op jit(solution)/shard_map/mul | solution.py:72
  59.1 54.5 %mul.181 = f32[128,16,1024]{2,1,0:T(8,128)} reshape(f32[2048,64,16]{2,1,0:T(8,128)} %mul.180) | data formatting | bytes 16777216 | tf_op jit(solution)/shard_map/mul | solution.py:72
  113.6 0.8 sine_negate_fusion
  114.3 22.0 %fusion.3 = f32[64,16,4096]{2,0,1:T(8,128)S(1)} fusion(bf16[64,16,4096]{2,0,1:T(8,128)(2,1)} %copy.46, bf16[64,15,4096]{2,0,1:T(8,128)(2,1)} %collective-permute-done, f32[16,1,4096]{2,0,1:T(8,128)S(1)} %bitcast.69), kind=kOutput, calls=%fused_computation.6 | convolution fusion | flops 813432832 | bytes 33292288 | tf_op jit(solution)/shard_map/conv_general_dilated | solution.py:60
  136.4 18.8 %copy.49 = f32[64,16,4096]{2,1,0:T(8,128)} copy(f32[64,16,4096]{2,0,1:T(8,128)S(1)} %fusion.3) | data formatting | bytes 33554432 | tf_op jit(solution)/shard_map/conv_general_dilated | solution.py:60
  155.2 27.0 %reshape.234 = f32[1024,64,64]{2,1,0:T(8,128)} reshape(f32[64,16,4096]{2,1,0:T(8,128)} %copy.49) | data formatting | bytes 33554432 | tf_op jit(solution)/shard_map/reshape | solution.py:26
  182.2 26.2 %copy.69 = f32[1024,64,64,1]{0,1,3,2:T(8,128)} copy(f32[1024,64,64,1]{2,1,0,3:T(8,128)} %bitcast.62) | data formatting | bytes 33554432 | tf_op jit(solution)/shard_map/reshape | solution.py:26
  208.5 33.7 %convolution_bitcast_fusion = f32[2,64,64,1024,1]{3,1,0,2,4:T(8,128)} fusion(f32[1024,64,64,1]{0,1,3,2:T(8,128)} %copy.69, f32[1,64,64]{2,1,0:T(8,128)S(1)} %copy-done.5, f32[1,64,64]{2,1,0:T(8,128)S(1)} %copy-done.6), kind=kOutput, calls=%fused_computation.10 | convolution fusion | flops 6442459136 | bytes 50364416 | tf_op jit(solution)/shard_map/qka,Rab->qkbR/dot_general | solution.py:31
  242.2 47.6 %fusion.7 = f32[2,32,64,1024]{3,1,0,2:T(8,128)} fusion(f32[2,32,64,2,64]{4,1,3,0,2:T(8,128)S(1)} %copy-done.1, f32[2,64,64,1024,1]{3,1,0,2,4:T(8,128)} %convolution_bitcast_fusion), kind=kOutput, calls=%fused_computation.11 | convolution fusion | flops 6442450944 | bytes 52428800 | tf_op jit(solution)/shard_map/qjksb,skbR->qjkR/dot_general | solution.py:43
  289.7 15.6 %copy.55 = f32[2,32,64,1024]{3,2,1,0:T(8,128)S(1)} copy(f32[2,32,64,1024]{3,1,0,2:T(8,128)} %fusion.7) | data formatting | bytes 33554432 | tf_op jit(solution)/shard_map/qjksb,skbR->qjkR/transpose | solution.py:43
  305.4 5.1 multiply_convert_fusion
  310.5 8.5 copy.57
  319.1 10.1 %all-to-all-start = ((bf16[2,128,16,1024]{3,2,0,1:T(8,128)(2,1)}), bf16[2,128,16,1024]{3,2,0,1:T(8,128)(2,1)}, u32[]{:S(2)}, u32[]{:S(2)}) async-start(bf16[2,128,16,1024]{3,2,0,1:T(8,128)(2,1)} %copy.57), calls=%async_computation | async-start | bytes 16777216 | tf_op jit(solution)/shard_map/all_to_all | solution.py:75
  329.2 0.6 shift-left_or_fusion
  329.8 0.8 iota_compare_fusion
  330.6 100.1 %all-to-all-done = bf16[2,128,16,1024]{3,2,0,1:T(8,128)(2,1)} async-done(((bf16[2,128,16,1024]{3,2,0,1:T(8,128)(2,1)}), bf16[2,128,16,1024]{3,2,0,1:T(8,128)(2,1)}, u32[]{:S(2)}, u32[]{:S(2)}) %all-to-all-start) | async-done | bytes 8388640 | tf_op jit(solution)/shard_map/all_to_all | solution.py:75
  430.6 62.1 %reshape.251 = bf16[2,8,16,16,64,16]{5,4,3,0,2,1:T(8,128)(2,1)} reshape(bf16[2,128,16,1024]{3,2,0,1:T(8,128)(2,1)} %all-to-all-done) | data formatting | bytes 16777216 | tf_op jit(solution)/shard_map/reshape | solution.py:76
  492.7 56.9 %copy.59 = bf16[2,8,16,16,64,16]{4,5,2,1,3,0:T(8,128)(2,1)} copy(bf16[2,8,16,16,64,16]{5,4,3,0,2,1:T(8,128)(2,1)} %reshape.251) | data formatting | bytes 16777216 | tf_op jit(solution)/shard_map/reshape | solution.py:76
  549.6 57.9 %copy.60 = bf16[2,16,8,64,16,16]{3,2,5,4,1,0:T(8,128)(2,1)} copy(bf16[2,16,8,64,16,16]{5,3,1,0,4,2:T(8,128)(2,1)} %bitcast.18) | data formatting | bytes 16777216 | tf_op jit(solution)/shard_map/transpose | solution.py:77
  607.5 22.5 %reshape.236 = bf16[2,16,512,256]{2,3,1,0:T(8,128)(2,1)} reshape(bf16[2,16,8,64,16,16]{3,2,5,4,1,0:T(8,128)(2,1)} %copy.60) | data formatting | bytes 16777216 | tf_op jit(solution)/shard_map/reshape | solution.py:77
  630.0 16.5 %convolution_bitcast_fusion.1 = f32[16,512,512]{2,1,0:T(8,128)} fusion(bf16[2,16,512,256]{2,3,1,0:T(8,128)(2,1)} %reshape.236), kind=kOutput, calls=%fused_computation.12 | convolution fusion | flops 4294967296 | bytes 25165824 | tf_op jit(solution)/shard_map/rcnt,rcmt->cnm/dot_general | solution.py:81
  646.4 11.7 %fusion.44 = (bf16[1,16,8,64,16,16]{3,5,4,2,1,0:T(8,128)(2,1)}, bf16[1,16,8,64,16,16]{3,5,4,2,1,0:T(8,128)(2,1)}) fusion(bf16[2,16,8,64,16,16]{3,5,4,2,1,0:T(8,128)(2,1)} %bitcast.63), kind=kLoop, calls=%fused_computation.70 | loop fusion | flops 2097152 | bytes 16777216 | tf_op jit(solution)/shard_map/slice | solution.py:80
  658.2 20.2 %copy.64 = bf16[1,16,8,64,16,16]{3,2,5,4,1,0:T(8,128)(2,1)} copy(bf16[1,16,8,64,16,16]{3,5,4,2,1,0:T(8,128)(2,1)} %get-tuple-element.6) | data formatting | bytes 8388608 | tf_op jit(solution)/shard_map/neg | solution.py:80
  678.4 11.8 %neg.47 = bf16[1,16,512,256]{2,3,1,0:T(8,128)(2,1)} reshape(bf16[1,16,8,64,16,16]{3,2,5,4,1,0:T(8,128)(2,1)} %copy.64) | data formatting | bytes 8388608 | tf_op jit(solution)/shard_map/neg | solution.py:80
  690.2 6.3 copy.66
  696.5 20.2 %copy.63 = bf16[1,16,8,64,16,16]{3,2,5,4,1,0:T(8,128)(2,1)} copy(bf16[1,16,8,64,16,16]{3,5,4,2,1,0:T(8,128)(2,1)} %get-tuple-element.5) | data formatting | bytes 8388608 | tf_op jit(solution)/shard_map/slice | solution.py:80
  716.8 11.8 %slice.15 = bf16[1,16,512,256]{2,3,1,0:T(8,128)(2,1)} reshape(bf16[1,16,8,64,16,16]{3,2,5,4,1,0:T(8,128)(2,1)} %copy.63) | data formatting | bytes 8388608 | tf_op jit(solution)/shard_map/slice | solution.py:80
  728.6 6.3 copy.65
  734.9 61.6 %copy.68 = f32[16,512,512]{0,2,1:T(8,128)} copy(f32[16,512,512]{2,1,0:T(8,128)} %convolution_bitcast_fusion.1) | data formatting | bytes 33554432 | tf_op jit(solution)/shard_map/rcnt,rcmt->cnm/dot_general | solution.py:81
  796.4 5.5 gather_fusion
  802.0 0.1 reduce_sum.9
  802.1 21.9 %psum.14 = f32[512]{0:T(512)S(1)} all-reduce(f32[512]{0:T(512)S(1)} %reduce_sum.9), channel_id=1, replica_groups=mesh['stn'=8,'tm'=16] {'stn'}, use_global_device_ids=true, to_apply=%region_1.2 | all-reduce | flops 512 | bytes 4096 | tf_op jit(solution)/shard_map/psum | solution.py:86
  824.0 30.0 %psum.15 = f32[512]{0:T(512)S(1)} all-reduce(f32[512]{0:T(512)S(1)} %psum.14), channel_id=1, replica_groups=mesh['stn'=8,'tm'=16] {'tm'}, use_global_device_ids=true, to_apply=%region_2.3 | all-reduce | flops 512 | bytes 4096 | tf_op jit(solution)/shard_map/psum | solution.py:86
  854.0 0.1 multiply_multiply_fusion
  854.2 18.9 %fusion.2 = f32[16,512,512]{2,1,0:T(8,128)} fusion(f32[16,512,512]{2,1,0:T(8,128)} %convolution_bitcast_fusion.1, bf16[1,16,512,256]{3,2,0,1:T(8,128)(2,1)} %copy.66, bf16[1,16,512,256]{3,2,0,1:T(8,128)(2,1)} %copy.65, bf16[2,16,512,256]{2,3,1,0:T(8,128)(2,1)} %reshape.236, f32[512,512]{1,0:T(8,128)S(1)} %multiply_multiply_fusion, ...), kind=kOutput, calls=%fused_computation.4 | convolution fusion | flops 4307550208 | bytes 51642368 | tf_op jit(solution)/shard_map/rcnt,rcmt->cnm/dot_general | solution.py:82
  (25 shorter events, 0.1 us)
Async XLA Ops:
  18.8 18.0 %copy-start.4 = (f32[16,4096]{1,0:T(8,128)S(1)}, f32[16,4096]{1,0:T(8,128)}, u32[]{:S(2)}) copy-start(f32[16,4096]{1,0:T(8,128)} %param.4) | copy-start | bytes 786436
  18.8 18.5 %copy-start.3 = (f32[64,2048]{1,0:T(8,128)S(1)}, f32[64,2048]{1,0:T(8,128)}, u32[]{:S(2)}) copy-start(f32[64,2048]{1,0:T(8,128)} %param.5) | copy-start | bytes 1572868
  18.8 95.6 %collective-permute-start = (bf16[64,15,4096]{2,0,1:T(8,128)(2,1)}, bf16[64,15,4096]{2,0,1:T(8,128)(2,1)}, u32[]{:S(2)}, u32[]{:S(2)}) collective-permute-start(bf16[64,15,4096]{2,0,1:T(8,128)(2,1)} %slice.19), channel_id=1, source_target_pairs={{0,1},{1,2},{2,3},{3,4},{4,5},{5,6},{6,7},{7,8},{8,9},{9,10},{10,1... | collective-permute-start | bytes 23592968 | tf_op jit(solution)/shard_map/ppermute | solution.py:11
  182.2 26.2 %copy-start.5 = (f32[1,64,64]{2,1,0:T(8,128)S(1)}, f32[1,64,64]{2,1,0:T(8,128)}, u32[]{:S(2)}) copy-start(f32[1,64,64]{2,1,0:T(8,128)} %get-tuple-element.15) | copy-start | bytes 49156
  182.2 26.2 %copy-start.6 = (f32[1,64,64]{2,1,0:T(8,128)S(1)}, f32[1,64,64]{2,1,0:T(8,128)}, u32[]{:S(2)}) copy-start(f32[1,64,64]{2,1,0:T(8,128)} %get-tuple-element.16) | copy-start | bytes 49156
  208.5 33.7 %copy-start.1 = (f32[2,32,64,2,64]{4,1,3,0,2:T(8,128)S(1)}, f32[2,32,64,2,64]{4,1,3,0,2:T(8,128)}, u32[]{:S(2)}) copy-start(f32[2,32,64,2,64]{4,1,3,0,2:T(8,128)} %copy.54) | copy-start | bytes 6291460
  208.5 96.9 %slice-start = ((s8[8388608]{0:T(1024)(128)(4,1)}), s8[4194304]{0:T(1024)(128)(4,1)S(1)}, s32[]{:S(2)}) async-start(s8[8388608]{0:T(1024)(128)(4,1)} %bitcast.66), calls=%async_computation.1 | async-start | bytes 8388608
  242.2 63.2 %slice-start.1 = ((s8[8388608]{0:T(1024)(128)(4,1)}), s8[4194304]{0:T(1024)(128)(4,1)S(1)}, s32[]{:S(2)}) async-start(s8[8388608]{0:T(1024)(128)(4,1)} %bitcast.66), calls=%async_computation.2 | async-start | bytes 8388608
  319.1 111.6 %all-to-all-start = ((bf16[2,128,16,1024]{3,2,0,1:T(8,128)(2,1)}), bf16[2,128,16,1024]{3,2,0,1:T(8,128)(2,1)}, u32[]{:S(2)}, u32[]{:S(2)}) async-start(bf16[2,128,16,1024]{3,2,0,1:T(8,128)(2,1)} %copy.57), calls=%async_computation | async-start | bytes 16777216 | tf_op jit(solution)/shard_map/all_to_all | solution.py:75
  734.9 61.6 %copy-start = (s32[512,1]{0,1:T(1,128)S(1)}, s32[512,1]{0,1:T(1,128)}, u32[]{:S(2)}) copy-start(s32[512,1]{0,1:T(1,128)} %shift-left_or_fusion) | copy-start | bytes 6148
  734.9 119.3 %copy-start.2 = (pred[512,512]{1,0:T(8,128)(4,1)S(1)}, pred[512,512]{1,0:T(8,128)(4,1)}, u32[]{:S(2)}) copy-start(pred[512,512]{1,0:T(8,128)(4,1)} %iota_compare_fusion) | copy-start | bytes 786436
